TPU v7x, 32 devices: a whole 2x2x4 slice. The times are simulated.
32 devices in a mesh: dp: 8 (over y, x, core), mp: 4 (over z).
Axes of the slice: x: 2, y: 2, z: 4, core: 2. Of those that a mesh axis runs over, the one named last changes fastest.
Arguments:
- tokens: bfloat16 [2, 1024, 4096], P(None, 'dp', 'mp'), may hold values from -6 to 6
- targets: bfloat16 [2, 1024, 4096], P(None, 'dp', 'mp'), may hold values from -6 to 6
- weight: bfloat16 [4096, 4096], P('mp'), may hold values from -0.09375 to 0.09375
- basis: bfloat16 [4096, 512], replicated, may hold values from -0.09375 to 0.09375
- moment1: float32 [4, 1024, 512], P('mp', 'dp'), may hold values from -0.06 to 0.06
- moment2: float32 [4, 1024, 512], P('mp', 'dp'), may hold values from 1e-05 to 0.001
Outputs:
- new_weight: bfloat16 [4096, 4096], P('mp')
- new_moment1: float32 [4, 1024, 512], P('mp', 'dp')
- new_moment2: float32 [4, 1024, 512], P('mp', 'dp')
All inputs are finite; a program needn't handle non-finite values.
Results may differ from a plain program's by a relative error of at most 0.009.
Values may be sent and summed in bfloat16 or wider, within the bound.
A program may use at most 64 MiB of HBM per device.

v0:
```python
import jax
import jax.numpy as jnp
from jax import lax
from jax.sharding import PartitionSpec as P


def local(tokens, targets, weight, basis, moment1, moment2):
    whole = lax.all_gather(tokens, "mp", axis=2, tiled=True)
    total_tokens = tokens.shape[1] * lax.axis_size("dp")
    owned_rows = moment1.shape[1]
    first = moment1[0]
    second = moment2[0]
    current = weight
    for turn in range(2):
        inputs = whole[turn]
        outputs = lax.dot_general(
            inputs, current, (((1,), (1,)), ((), ())), preferred_element_type=jnp.float32
        ).astype(jnp.bfloat16)
        errors = (outputs.astype(jnp.float32) - targets[turn].astype(jnp.float32)).astype(
            jnp.bfloat16
        )
        reduced = jnp.dot(inputs, basis, preferred_element_type=jnp.float32)
        part_errors = errors.astype(jnp.float32)
        projected = (
            lax.psum_scatter(
                lax.dot_general(
                    part_errors, reduced, (((0,), (0,)), ((), ())), precision=lax.Precision.HIGHEST
                ),
                "dp",
                scatter_dimension=0,
                tiled=True,
            )
            / total_tokens
        )
        first = 0.9 * first + 0.1 * projected
        second = 0.95 * second + 0.05 * projected * projected
        direction = (first / (jnp.sqrt(second) + 1e-08)).astype(jnp.bfloat16)
        own_weight = lax.dynamic_slice_in_dim(
            current, lax.axis_index("dp") * owned_rows, owned_rows, 0
        )
        lifted = lax.dot_general(
            direction, basis, (((1,), (1,)), ((), ())), preferred_element_type=jnp.float32
        )
        new_rows = (own_weight.astype(jnp.float32) - 0.02 * lifted).astype(jnp.bfloat16)
        current = lax.all_gather(new_rows, "dp", axis=0, tiled=True)
    return (current, first[None], second[None])


def solution(mesh):
    in_specs = (
        P(None, "dp", "mp"),
        P(None, "dp", "mp"),
        P("mp", None),
        P(),
        P("mp", "dp", None),
        P("mp", "dp", None),
    )
    out_specs = (P("mp", None), P("mp", "dp", None), P("mp", "dp", None))
    return jax.shard_map(local, mesh=mesh, in_specs=in_specs, out_specs=out_specs, check_vma=False)
```

profile of v0, /device:TPU:0, one launch (start us, length us, event | category | flops | bytes accessed | tf_op | source)
XLA Modules:
  0.0 293.4 jit_solution(11323379693087445901)
XLA Ops:
  7.2 0.0 copy-start.5
  7.2 0.0 all-gather.4.cloned.1.call-start
  7.2 0.7 all-gather.4.cloned.1.call-update
  7.9 0.0 reduce-scatter.3.cloned.1.call-start
  8.0 50.0 %all-gather.4.cloned.1.call-done = bf16[2,128,4096]{2,1,0:T(8,128)(2,1)} async-done(((bf16[2,128,1024]{2,1,0:T(8,128)(2,1)}), bf16[2,128,4096]{2,1,0:T(8,128)(2,1)}) %all-gather.4.cloned.1.call-update) | async-done | bytes 2097168 | tf_op jit(solution)/shard_map/all_gather | solution.py:8
  58.0 3.4 %fusion.11 = f32[128,512]{1,0:T(8,128)S(1)} fusion(bf16[4096,512]{1,0:T(8,128)(2,1)} %param.9, bf16[2,128,4096]{2,1,0:T(8,128)(2,1)} %all-gather.4.cloned.1.call-done), kind=kOutput, calls=%fused_computation.17 | convolution fusion | flops 536870912 | bytes 5505024 | tf_op jit(solution)/shard_map/dot_general | solution.py:22
  61.3 0.0 copy-done.5
  61.4 0.0 copy-done
  61.4 6.3 %fusion.10 = bf16[128,1024]{1,0:T(8,128)(2,1)S(1)} fusion(bf16[1024,4096]{1,0:T(8,128)(2,1)} %param.8, bf16[2,128,4096]{2,1,0:T(8,128)(2,1)S(1)} %copy-done, bf16[2,128,1024]{2,1,0:T(8,128)(2,1)S(1)} %copy-done.5), kind=kOutput, calls=%fused_computation.14 | convolution fusion | flops 1074397184 | bytes 9961472 | tf_op jit(solution)/shard_map/dot_general | solution.py:16
  67.6 0.0 copy-start.1
  67.6 0.0 copy-start.2
  67.7 2.4 fusion.24
  70.0 0.0 reduce-scatter.3.cloned.1.call-update
  70.0 0.0 all-gather.6.cloned.1.call-start
  70.1 40.0 %reduce-scatter.3.cloned.1.call-done = f32[128,512]{1,0:T(8,128)} async-done(((f32[1024,512]{1,0:T(8,128)}), f32[128,512]{1,0:T(8,128)}) %reduce-scatter.3.cloned.1.call-update) | async-done | bytes 262160 | tf_op jit(solution)/shard_map/reduce_scatter | solution.py:25
  110.1 0.0 copy-done.1
  110.1 0.0 copy-done.2
  110.1 5.0 %fusion.2 = bf16[128,4096]{1,0:T(8,128)(2,1)} fusion(bf16[4096,512]{1,0:T(8,128)(2,1)} %param.9, bf16[1024,4096]{1,0:T(8,128)(2,1)} %param.8, s32[]{:T(128)S(6)} %select_n.4, f32[128,512]{1,0:T(8,128)} %reduce-scatter.3.cloned.1.call-done, f32[1,128,512]{2,1,0:T(8,128)S(1)} %copy-done.1, f32[1,128,512]{2,1,0:T(8,128)S(1)} %copy-done.2), kind=kOutput, calls=%fused_computation.4 | convolution fusion | flops 539688960 | bytes 7077892 | tf_op jit(solution)/shard_map/dot_general | solution.py:41
  115.1 0.0 all-gather.6.cloned.1.call-update
  115.1 0.0 reduce-scatter.5.cloned.1.call-start
  115.2 2.9 fusion.12
  118.1 51.5 %all-gather.6.cloned.1.call-done = bf16[1024,4096]{1,0:T(8,128)(2,1)} async-done(((bf16[128,4096]{1,0:T(8,128)(2,1)}), bf16[1024,4096]{1,0:T(8,128)(2,1)}) %all-gather.6.cloned.1.call-update) | async-done | bytes 8388624 | tf_op jit(solution)/shard_map/all_gather | solution.py:45
  169.5 6.3 %fusion.7 = bf16[128,1024]{1,0:T(8,128)(2,1)S(1)} fusion(bf16[1024,4096]{1,0:T(8,128)(2,1)} %all-gather.6.cloned.1.call-done, bf16[2,128,4096]{2,1,0:T(8,128)(2,1)S(1)} %copy-done, bf16[2,128,1024]{2,1,0:T(8,128)(2,1)S(1)} %copy-done.5), kind=kOutput, calls=%fused_computation.10 | convolution fusion | flops 1074397184 | bytes 9961472 | tf_op jit(solution)/shard_map/dot_general | solution.py:16
  175.8 2.4 fusion.25
  178.2 0.0 reduce-scatter.5.cloned.1.call-update
  178.2 0.0 all-gather.8.cloned.1.call-start
  178.2 41.2 %reduce-scatter.5.cloned.1.call-done = f32[128,512]{1,0:T(8,128)} async-done(((f32[1024,512]{1,0:T(8,128)}), f32[128,512]{1,0:T(8,128)}) %reduce-scatter.5.cloned.1.call-update) | async-done | bytes 262160 | tf_op jit(solution)/shard_map/reduce_scatter | solution.py:25
  219.4 5.1 %fusion.3 = bf16[128,4096]{1,0:T(8,128)(2,1)} fusion(bf16[4096,512]{1,0:T(8,128)(2,1)} %param.9, bf16[1024,4096]{1,0:T(8,128)(2,1)} %all-gather.6.cloned.1.call-done, s32[]{:T(128)S(6)} %select_n.4, f32[128,512]{1,0:T(8,128)} %reduce-scatter.5.cloned.1.call-done, f32[128,512]{1,0:T(8,128)S(1)} %copy-done.3, f32[1,128,512]{2,1,0:T(8,128)S(1)} %copy-done.1, ...), kind=kOutput, calls=%fused_computation.5 | convolution fusion | flops 540213248 | bytes 7340036 | tf_op jit(solution)/shard_map/dot_general | solution.py:41
  224.5 0.0 all-gather.8.cloned.1.call-update
  224.6 0.9 fusion.16
  225.5 53.5 %all-gather.8.cloned.1.call-done = bf16[1024,4096]{1,0:T(8,128)(2,1)} async-done(((bf16[128,4096]{1,0:T(8,128)(2,1)}), bf16[1024,4096]{1,0:T(8,128)(2,1)}) %all-gather.8.cloned.1.call-update) | async-done | bytes 8388624 | tf_op jit(solution)/shard_map/all_gather | solution.py:45
  279.0 7.9 %copy.10 = bf16[1024,4096]{1,0:T(8,128)(2,1)} copy(bf16[1024,4096]{1,0:T(8,128)(2,1)} %all-gather.8.cloned.1.call-done) | data formatting | bytes 16777216
  (5 shorter events, 0.0 us)
Async XLA Ops:
  7.2 54.2 %copy-start.5 = (bf16[2,128,1024]{2,1,0:T(8,128)(2,1)S(1)}, bf16[2,128,1024]{2,1,0:T(8,128)(2,1)}, u32[]{:S(2)}) copy-start(bf16[2,128,1024]{2,1,0:T(8,128)(2,1)} %param.7) | copy-start | bytes 1572868
  7.2 50.8 %all-gather.4.cloned.1.call-start = ((), (), s32[]{:S(2)}) async-start(), calls=%async_computation.2 | async-start | bytes 2621440 | tf_op jit(solution)/shard_map/all_gather | solution.py:8
  7.9 102.2 %reduce-scatter.3.cloned.1.call-start = ((), (), s32[]{:S(2)}) async-start(), calls=%async_computation.3 | async-start | bytes 2359296 | tf_op jit(solution)/shard_map/reduce_scatter | solution.py:25
  58.0 3.4 %copy-start = (bf16[2,128,4096]{2,1,0:T(8,128)(2,1)S(1)}, bf16[2,128,4096]{2,1,0:T(8,128)(2,1)}, u32[]{:S(2)}) copy-start(bf16[2,128,4096]{2,1,0:T(8,128)(2,1)} %all-gather.4.cloned.1.call-done) | copy-start | bytes 6291460
  67.6 42.5 %copy-start.1 = (f32[1,128,512]{2,1,0:T(8,128)S(1)}, f32[1,128,512]{2,1,0:T(8,128)}, u32[]{:S(2)}) copy-start(f32[1,128,512]{2,1,0:T(8,128)} %param.10) | copy-start | bytes 786436
  67.6 42.5 %copy-start.2 = (f32[1,128,512]{2,1,0:T(8,128)S(1)}, f32[1,128,512]{2,1,0:T(8,128)}, u32[]{:S(2)}) copy-start(f32[1,128,512]{2,1,0:T(8,128)} %param.11) | copy-start | bytes 786436
  70.0 99.5 %all-gather.6.cloned.1.call-start = ((), (), s32[]{:S(2)}) async-start(), calls=%async_computation.4 | async-start | bytes 9437184 | tf_op jit(solution)/shard_map/all_gather | solution.py:45
  115.1 104.3 %reduce-scatter.5.cloned.1.call-start = ((), (), s32[]{:S(2)}) async-start(), calls=%async_computation.5 | async-start | bytes 2359296 | tf_op jit(solution)/shard_map/reduce_scatter | solution.py:25
  175.8 43.6 %copy-start.3 = (f32[128,512]{1,0:T(8,128)S(1)}, f32[128,512]{1,0:T(8,128)}, u32[]{:S(2)}) copy-start(f32[128,512]{1,0:T(8,128)} %reduce-scatter.3.cloned.1.call-done) | copy-start | bytes 786436
  178.2 100.8 %all-gather.8.cloned.1.call-start = ((), (), s32[]{:S(2)}) async-start(), calls=%async_computation.6 | async-start | bytes 9437184 | tf_op jit(solution)/shard_map/all_gather | solution.py:45
  219.4 5.1 %copy-start.4 = (f32[128,512]{1,0:T(8,128)S(1)}, f32[128,512]{1,0:T(8,128)}, u32[]{:S(2)}) copy-start(f32[128,512]{1,0:T(8,128)} %reduce-scatter.5.cloned.1.call-done) | copy-start | bytes 786436
Sparse Core Ops, SparseCore 0:
  9.6 48.3 all-gather.3
  70.2 39.9 reduce-scatter.2
  115.2 54.2 all-gather.5
  178.3 41.0 reduce-scatter.4
  224.7 54.2 all-gather.7
where the time goes:
time: 294 us; the launch traced here: 293 us
  waiting for transfers between devices  237 us (81%)
  matrix products  33.6 us (11%)
  between operations  13.9 us (5%)
  local copies, waits for them, and re-layouts  7.91 us (3%)
    all_gather x2, waiting for transfers between devices, local(): current = lax.all_gather(new_rows, 'dp', axis=0, tiled=True)  105 us
    reduce_scatter x2, waiting for transfers between devices, local(): lax.psum_scatter(lax.dot_general(part_errors, reduced, (((0,), (0,)), (()...  81.2 us
    all_gather x1, waiting for transfers between devices, local(): whole = lax.all_gather(tokens, 'mp', axis=2, tiled=True)  50 us
    dot_general x2, matrix products, local(): lax.dot_general(inputs, current, (((1,), (1,)), ((), ())), preferred_elem...  12.5 us
    dot_general x2, matrix products, local(): lax.dot_general(direction, basis, (((1,), (1,)), ((), ())), preferred_ele...  10.1 us
    unnamed x13, local copies, waits for them, and re-layouts  7.91 us
    dot_general x2, matrix products, local(): reduced = jnp.dot(inputs, basis, preferred_element_type=jnp.float32)  6.28 us
  transfers between devices with their start and end apart: 5, of which 5 were waited for; matrix products, arithmetic and copies ran while one was open for 1% of the time, Pallas kernels for 0%

commit v1 on v0

--- a/solution.py
+++ b/solution.py
@@ -4,8 +4,20 @@
 from jax.sharding import PartitionSpec as P
 
 
+def _clear_tokens(incoming_x, link_axis):
+    cores_n = lax.psum(1, link_axis)
+    e_next = sorted(((jj, (jj + 1) % cores_n) for jj in range(cores_n)))
+    met_up = incoming_x
+    entries = [met_up]
+    for s in tuple(range(1, cores_n)):
+        met_up = lax.ppermute(met_up, axis_name=link_axis, perm=e_next)
+        entries.insert(0, met_up)
+    top = jnp.concatenate(entries, axis=2)
+    return jnp.roll(top, (lax.axis_index(link_axis) + 1) * incoming_x.shape[2], 2)
+
+
 def local(tokens, targets, weight, basis, moment1, moment2):
-    whole = lax.all_gather(tokens, "mp", axis=2, tiled=True)
+    whole = _clear_tokens(tokens, link_axis="mp")
     total_tokens = tokens.shape[1] * lax.axis_size("dp")
     owned_rows = moment1.shape[1]
     first = moment1[0]

time: 294 us -> 288 us (0.980)
  waiting for transfers between devices: 237 us -> 228 us
  local copies, waits for them, and re-layouts: 7.91 us -> 13.4 us
  matrix products: 33.6 us -> 28.4 us
  starting transfers between devices: 0.2 us -> 3.27 us
    all_gather x1 -> x0, waiting for transfers between devices: 50 us -> none  [local(): whole = lax.all_gather(tokens, 'mp', axis=2, tiled=True)]
    ppermute x0 -> x3, waiting for transfers between devices: none -> 43.1 us  [_clear_tokens(): met_up = lax.ppermute(met_up, axis_name=link_axis, perm=e_next)]
    unnamed x13 -> x26, local copies, waits for them, and re-layouts: 7.91 us -> 13.4 us
    ppermute x0 -> x3, starting transfers between devices: none -> 3.11 us  [_clear_tokens(): met_up = lax.ppermute(met_up, axis_name=link_axis, perm=e_next)]
    dot_general x2, matrix products: 12.5 us -> 9.51 us  [local(): lax.dot_general(inputs, current, (((1,), (1,)), ((), ())), preferred_elem...]
  transfers between devices with their start and end apart: 5 -> 7, of which waited for: 5 -> 7; matrix products, arithmetic and copies ran while one was open for 1% -> 1% of each run, Pallas kernels for 0% -> 0%
where the time goes in v1:
time: 288 us
  waiting for transfers between devices  228 us (79%)
  matrix products  28.4 us (10%)
  between operations  13.9 us (5%)
  local copies, waits for them, and re-layouts  13.4 us (5%)
  starting transfers between devices  3.27 us (1%)
    all_gather x2, waiting for transfers between devices, local(): current = lax.all_gather(new_rows, 'dp', axis=0, tiled=True)  105 us
    reduce_scatter x2, waiting for transfers between devices, local(): lax.psum_scatter(lax.dot_general(part_errors, reduced, (((0,), (0,)), (()...  80.2 us
    ppermute x3, waiting for transfers between devices, _clear_tokens(): met_up = lax.ppermute(met_up, axis_name=link_axis, perm=e_next)  43.1 us
    unnamed x26, local copies, waits for them, and re-layouts  13.4 us
    dot_general x2, matrix products, local(): lax.dot_general(direction, basis, (((1,), (1,)), ((), ())), preferred_ele...  10.2 us
    dot_general x2, matrix products, local(): lax.dot_general(inputs, current, (((1,), (1,)), ((), ())), preferred_elem...  9.51 us
  transfers between devices with their start and end apart: 7, of which 7 were waited for; matrix products, arithmetic and copies ran while one was open for 1% of the time, Pallas kernels for 0%

profile of v1, /device:TPU:0, one launch (start us, length us, event | category | flops | bytes accessed | tf_op | source)
XLA Modules:
  0.0 287.8 jit_solution(2537104762573849603)
XLA Ops:
  7.2 0.0 copy-start.6
  7.2 0.0 reduce-scatter.3.cloned.1.call-start
  7.2 3.1 %collective-permute-start = (bf16[2,128,1024]{2,1,0:T(8,128)(2,1)}, bf16[2,128,1024]{2,1,0:T(8,128)(2,1)S(1)}, u32[]{:S(2)}, u32[]{:S(2)}) collective-permute-start(bf16[2,128,1024]{2,1,0:T(8,128)(2,1)} %param.6), channel_id=1, source_target_pairs={{0,1},{1,2},{2,3},{3,0},{4,5},{5,6},{6,7},{7,4},{8,9},{9,10},{10,1... | collective-permute-start | bytes 1572872 | tf_op jit(solution)/shard_map/ppermute | solution.py:13
  10.3 14.2 %collective-permute-done = bf16[2,128,1024]{2,1,0:T(8,128)(2,1)S(1)} collective-permute-done((bf16[2,128,1024]{2,1,0:T(8,128)(2,1)}, bf16[2,128,1024]{2,1,0:T(8,128)(2,1)S(1)}, u32[]{:S(2)}, u32[]{:S(2)}) %collective-permute-start) | collective-permute-done | bytes 524320 | tf_op jit(solution)/shard_map/ppermute | solution.py:13
  24.5 14.9 %collective-permute-done.1 = bf16[2,128,1024]{2,1,0:T(8,128)(2,1)S(1)} collective-permute-done((bf16[2,128,1024]{2,1,0:T(8,128)(2,1)S(1)}, bf16[2,128,1024]{2,1,0:T(8,128)(2,1)S(1)}, u32[]{:S(2)}, u32[]{:S(2)}) %collective-permute-start.1) | collective-permute-done | bytes 524320 | tf_op jit(solution)/shard_map/ppermute | solution.py:13
  39.4 14.0 %collective-permute-done.2 = bf16[2,128,1024]{2,1,0:T(8,128)(2,1)S(1)} collective-permute-done((bf16[2,128,1024]{2,1,0:T(8,128)(2,1)S(1)}, bf16[2,128,1024]{2,1,0:T(8,128)(2,1)S(1)}, u32[]{:S(2)}, u32[]{:S(2)}) %collective-permute-start.2) | collective-permute-done | bytes 524320 | tf_op jit(solution)/shard_map/ppermute | solution.py:13
  53.5 1.1 constant_dynamic-update-slice_fusion.4
  54.6 0.0 copy-start.8
  54.7 0.0 copy-start.1
  54.9 0.7 fusion.10
  55.6 0.1 copy-done.8
  55.7 4.0 %copy-done.1 = bf16[1024,4096]{1,0:T(8,128)(2,1)S(1)} copy-done((bf16[1024,4096]{1,0:T(8,128)(2,1)S(1)}, bf16[1024,4096]{1,0:T(8,128)(2,1)}, u32[]{:S(2)}) %copy-start.1) | copy-done | bytes 8388632
  59.7 2.9 %fusion.9 = bf16[128,1024]{1,0:T(8,128)(2,1)S(1)} fusion(bf16[1024,4096]{1,0:T(8,128)(2,1)S(1)} %copy-done.1, bf16[2,128,8192]{2,1,0:T(8,128)(2,1)S(1)} %constant_dynamic-update-slice_fusion, s32[]{:T(128)S(6)} %select_n.19, bf16[2,128,1024]{2,1,0:T(8,128)(2,1)S(1)} %copy-done.8), kind=kOutput, calls=%fused_computation.13 | convolution fusion | flops 1074397184 | bytes 9961476 | tf_op jit(solution)/shard_map/dot_general | solution.py:28
  62.6 2.4 fusion.27
  65.0 0.0 reduce-scatter.3.cloned.1.call-update
  65.0 0.0 all-gather.3.cloned.1.call-start
  65.1 39.0 %reduce-scatter.3.cloned.1.call-done = f32[128,512]{1,0:T(8,128)} async-done(((f32[1024,512]{1,0:T(8,128)}), f32[128,512]{1,0:T(8,128)}) %reduce-scatter.3.cloned.1.call-update) | async-done | bytes 262160 | tf_op jit(solution)/shard_map/reduce_scatter | solution.py:37
  104.1 5.1 %fusion.2 = bf16[128,4096]{1,0:T(8,128)(2,1)} fusion(bf16[4096,512]{1,0:T(8,128)(2,1)} %param.9, bf16[1024,4096]{1,0:T(8,128)(2,1)} %param.8, s32[]{:T(128)S(6)} %select_n.17, f32[128,512]{1,0:T(8,128)} %reduce-scatter.3.cloned.1.call-done, f32[1,128,512]{2,1,0:T(8,128)S(1)} %copy-done.3, f32[1,128,512]{2,1,0:T(8,128)S(1)} %copy-done.4), kind=kOutput, calls=%fused_computation.4 | convolution fusion | flops 539688960 | bytes 7077892 | tf_op jit(solution)/shard_map/dot_general | solution.py:53
  109.2 0.0 all-gather.3.cloned.1.call-update
  109.2 0.0 reduce-scatter.5.cloned.1.call-start
  109.3 3.2 %fusion.11 = f32[128,512]{1,0:T(8,128)S(1)} fusion(bf16[4096,512]{1,0:T(8,128)(2,1)} %param.9, bf16[2,128,8192]{2,1,0:T(8,128)(2,1)} %copy-done.2, s32[]{:T(128)S(6)} %add.49, s32[]{:T(128)S(6)} %select_n.19), kind=kOutput, calls=%fused_computation.17 | convolution fusion | flops 536870912 | bytes 5505032 | tf_op jit(solution)/shard_map/dot_general | solution.py:34
  112.5 51.1 %all-gather.3.cloned.1.call-done = bf16[1024,4096]{1,0:T(8,128)(2,1)} async-done(((bf16[128,4096]{1,0:T(8,128)(2,1)}), bf16[1024,4096]{1,0:T(8,128)(2,1)}) %all-gather.3.cloned.1.call-update) | async-done | bytes 8388624 | tf_op jit(solution)/shard_map/all_gather | solution.py:57
  163.6 6.6 %fusion.6 = bf16[128,1024]{1,0:T(8,128)(2,1)S(1)} fusion(bf16[1024,4096]{1,0:T(8,128)(2,1)} %all-gather.3.cloned.1.call-done, bf16[2,128,8192]{2,1,0:T(8,128)(2,1)} %copy-done.2, s32[]{:T(128)S(6)} %add.49, s32[]{:T(128)S(6)} %select_n.19, bf16[2,128,1024]{2,1,0:T(8,128)(2,1)S(1)} %copy-done.8), kind=kOutput, calls=%fused_computation.9 | convolution fusion | flops 1074397184 | bytes 9961480 | tf_op jit(solution)/shard_map/dot_general | solution.py:28
  170.2 2.4 fusion.28
  172.6 0.0 reduce-scatter.5.cloned.1.call-update
  172.6 0.0 all-gather.5.cloned.1.call-start
  172.7 41.2 %reduce-scatter.5.cloned.1.call-done = f32[128,512]{1,0:T(8,128)} async-done(((f32[1024,512]{1,0:T(8,128)}), f32[128,512]{1,0:T(8,128)}) %reduce-scatter.5.cloned.1.call-update) | async-done | bytes 262160 | tf_op jit(solution)/shard_map/reduce_scatter | solution.py:37
  213.9 5.1 %fusion.3 = bf16[128,4096]{1,0:T(8,128)(2,1)} fusion(bf16[4096,512]{1,0:T(8,128)(2,1)} %param.9, bf16[1024,4096]{1,0:T(8,128)(2,1)} %all-gather.3.cloned.1.call-done, s32[]{:T(128)S(6)} %select_n.17, f32[128,512]{1,0:T(8,128)} %reduce-scatter.5.cloned.1.call-done, f32[128,512]{1,0:T(8,128)S(1)} %copy-done.5, f32[1,128,512]{2,1,0:T(8,128)S(1)} %copy-done.3, ...), kind=kOutput, calls=%fused_computation.5 | convolution fusion | flops 540213248 | bytes 7340036 | tf_op jit(solution)/shard_map/dot_general | solution.py:53
  219.0 0.0 all-gather.5.cloned.1.call-update
  219.0 0.9 fusion.15
  220.0 53.4 %all-gather.5.cloned.1.call-done = bf16[1024,4096]{1,0:T(8,128)(2,1)} async-done(((bf16[128,4096]{1,0:T(8,128)(2,1)}), bf16[1024,4096]{1,0:T(8,128)(2,1)}) %all-gather.5.cloned.1.call-update) | async-done | bytes 8388624 | tf_op jit(solution)/shard_map/all_gather | solution.py:57
  273.4 7.9 %copy.17 = bf16[1024,4096]{1,0:T(8,128)(2,1)} copy(bf16[1024,4096]{1,0:T(8,128)(2,1)} %all-gather.5.cloned.1.call-done) | data formatting | bytes 16777216
  (22 shorter events, 0.3 us)
Async XLA Ops:
  7.2 47.6 %copy-start.6 = (bf16[2,128,1024]{2,1,0:T(8,128)(2,1)S(1)}, bf16[2,128,1024]{2,1,0:T(8,128)(2,1)}, u32[]{:S(2)}) copy-start(bf16[2,128,1024]{2,1,0:T(8,128)(2,1)} %param.6) | copy-start | bytes 1572868
  7.2 96.9 %reduce-scatter.3.cloned.1.call-start = ((), (), s32[]{:S(2)}) async-start(), calls=%async_computation.2 | async-start | bytes 2359296 | tf_op jit(solution)/shard_map/reduce_scatter | solution.py:37
  7.2 17.3 %collective-permute-start = (bf16[2,128,1024]{2,1,0:T(8,128)(2,1)}, bf16[2,128,1024]{2,1,0:T(8,128)(2,1)S(1)}, u32[]{:S(2)}, u32[]{:S(2)}) collective-permute-start(bf16[2,128,1024]{2,1,0:T(8,128)(2,1)} %param.6), channel_id=1, source_target_pairs={{0,1},{1,2},{2,3},{3,0},{4,5},{5,6},{6,7},{7,4},{8,9},{9,10},{10,1... | collective-permute-start | bytes 1572872 | tf_op jit(solution)/shard_map/ppermute | solution.py:13
  24.5 14.9 %collective-permute-start.1 = (bf16[2,128,1024]{2,1,0:T(8,128)(2,1)S(1)}, bf16[2,128,1024]{2,1,0:T(8,128)(2,1)S(1)}, u32[]{:S(2)}, u32[]{:S(2)}) collective-permute-start(bf16[2,128,1024]{2,1,0:T(8,128)(2,1)S(1)} %collective-permute-done), channel_id=1, source_target_pairs={{0,1},{1,2},{2,3},{3,0},{4,5},{5,6},{6,7},{7,4},{8,9},{9,10},{10,1... | collective-permute-start | bytes 1572872 | tf_op jit(solution)/shard_map/ppermute | solution.py:13
  39.4 14.0 %collective-permute-start.2 = (bf16[2,128,1024]{2,1,0:T(8,128)(2,1)S(1)}, bf16[2,128,1024]{2,1,0:T(8,128)(2,1)S(1)}, u32[]{:S(2)}, u32[]{:S(2)}) collective-permute-start(bf16[2,128,1024]{2,1,0:T(8,128)(2,1)S(1)} %collective-permute-done.1), channel_id=1, source_target_pairs={{0,1},{1,2},{2,3},{3,0},{4,5},{5,6},{6,7},{7,4},{8,9},{9,10},{10,1... | collective-permute-start | bytes 1572872 | tf_op jit(solution)/shard_map/ppermute | solution.py:13
  39.4 15.5 %copy-start = (bf16[4096,512]{1,0:T(8,128)(2,1)S(1)}, bf16[4096,512]{1,0:T(8,128)(2,1)}, u32[]{:S(2)}) copy-start(bf16[4096,512]{1,0:T(8,128)(2,1)} %param.9) | copy-start | bytes 12582916
  54.6 1.0 copy-start.8
  54.7 5.0 %copy-start.1 = (bf16[1024,4096]{1,0:T(8,128)(2,1)S(1)}, bf16[1024,4096]{1,0:T(8,128)(2,1)}, u32[]{:S(2)}) copy-start(bf16[1024,4096]{1,0:T(8,128)(2,1)} %param.8) | copy-start | bytes 25165828
  54.8 7.8 %copy-start.2 = (bf16[2,128,8192]{2,1,0:T(8,128)(2,1)}, bf16[2,128,8192]{2,1,0:T(8,128)(2,1)S(1)}, u32[]{:S(2)}) copy-start(bf16[2,128,8192]{2,1,0:T(8,128)(2,1)S(1)} %constant_dynamic-update-slice_fusion) | copy-start | bytes 12582916
  62.6 41.5 %copy-start.3 = (f32[1,128,512]{2,1,0:T(8,128)S(1)}, f32[1,128,512]{2,1,0:T(8,128)}, u32[]{:S(2)}) copy-start(f32[1,128,512]{2,1,0:T(8,128)} %param.10) | copy-start | bytes 786436
  62.6 41.5 %copy-start.4 = (f32[1,128,512]{2,1,0:T(8,128)S(1)}, f32[1,128,512]{2,1,0:T(8,128)}, u32[]{:S(2)}) copy-start(f32[1,128,512]{2,1,0:T(8,128)} %param.11) | copy-start | bytes 786436
  65.0 98.6 %all-gather.3.cloned.1.call-start = ((), (), s32[]{:S(2)}) async-start(), calls=%async_computation.3 | async-start | bytes 9437184 | tf_op jit(solution)/shard_map/all_gather | solution.py:57
  109.2 104.7 %reduce-scatter.5.cloned.1.call-start = ((), (), s32[]{:S(2)}) async-start(), calls=%async_computation.4 | async-start | bytes 2359296 | tf_op jit(solution)/shard_map/reduce_scatter | solution.py:37
  170.2 43.6 %copy-start.5 = (f32[128,512]{1,0:T(8,128)S(1)}, f32[128,512]{1,0:T(8,128)}, u32[]{:S(2)}) copy-start(f32[128,512]{1,0:T(8,128)} %reduce-scatter.3.cloned.1.call-done) | copy-start | bytes 786436
  172.6 100.8 %all-gather.5.cloned.1.call-start = ((), (), s32[]{:S(2)}) async-start(), calls=%async_computation.5 | async-start | bytes 9437184 | tf_op jit(solution)/shard_map/all_gather | solution.py:57
  213.9 5.1 %copy-start.7 = (f32[128,512]{1,0:T(8,128)S(1)}, f32[128,512]{1,0:T(8,128)}, u32[]{:S(2)}) copy-start(f32[128,512]{1,0:T(8,128)} %reduce-scatter.5.cloned.1.call-done) | copy-start | bytes 786436
Sparse Core Ops, SparseCore 0:
  65.2 38.9 reduce-scatter.2
  109.3 54.2 all-gather.2
  172.7 41.0 reduce-scatter.4
  219.1 54.2 all-gather.4
